TPU v7x, 256 devices: a whole 4x4x8 slice. The times are simulated.
256 devices in a mesh: seq: 64 (over z, y, core), grp: 4 (over x).
Axes of the slice: x: 4, y: 4, z: 8, core: 2. Of those that a mesh axis runs over, the one named last changes fastest.
Arguments:
- q_nope: bfloat16 [1024, 128, 128], P('seq', 'grp'), may hold values from -6 to 6
- q_rope: bfloat16 [1024, 128, 64], P('seq', 'grp'), may hold values from -256 to 256
- cache: bfloat16 [65536, 576], P('seq'), may hold values from -6 to 6
- w_uk: bfloat16 [128, 65536], P('grp', 'seq'), may hold values from -0.5 to 0.5
- w_uv: bfloat16 [128, 65536], P('grp', 'seq'), may hold values from -0.25 to 0.25
- d_out: bfloat16 [1024, 128, 128], P('seq', 'grp'), may hold values from -6 to 6
- sel: int32 [1024, 32], P('seq'), may hold values from 0 to 63, as said below
- slot_blocks: int32 [64, 64], P('seq'), may hold values from 0 to 15, as said below
Outputs:
- attn_out: bfloat16 [1024, 128, 128], P('seq', 'grp')
- d_q_nope: bfloat16 [1024, 128, 128], P('seq', 'grp')
- d_q_rope: bfloat16 [1024, 128, 64], P('seq', 'grp')
- d_cache: float32 [65536, 576], P('seq')
Inputs may be any that keep to these rules, and one draw needn't show every extreme that they name: `sel`: each row names 32 different places; place s stands for the block that the row's device asks of device s. `slot_blocks`: entry [r, s] is the index among device s's own blocks of the block that device r asks for in place s; the 1 entries of a row toward one device differ.
All inputs are finite; a program needn't handle non-finite values.
Results may differ from a plain program's by a relative error of at most 0.015.
Values may be sent and summed in bfloat16 or wider, within the bound.
A program may use at most 128 MiB of HBM per device.

v0:
```python
import math
import jax
import jax.numpy as jnp
from jax import lax
from jax.sharding import PartitionSpec as P

BLOCK_LEN = 64


def local(q_nope, q_rope, cache, w_uk, w_uv, d_out, sel, slot_blocks):
    peers = lax.axis_size("seq")
    queries, heads, nope = q_nope.shape
    rope = q_rope.shape[2]
    width = cache.shape[1]
    latent = width - rope
    value = d_out.shape[2]
    slot_total = slot_blocks.shape[1]
    per_peer = slot_total // peers
    own_blocks = cache.shape[0] // BLOCK_LEN
    scale = 1.0 / math.sqrt(nope + rope)
    gathered_k, gathered_v = (
        lax.all_gather(w_uk, "seq", axis=1, tiled=True),
        lax.all_gather(w_uv, "seq", axis=1, tiled=True),
    )
    weight_k = gathered_k.reshape(heads, nope, latent)
    weight_v = gathered_v.reshape(heads, latent, value)
    wanted = slot_blocks.reshape(peers, per_peer)
    asked = lax.all_to_all(wanted, "seq", split_axis=0, concat_axis=0, tiled=True)
    blocks = cache.reshape(own_blocks, BLOCK_LEN, width)
    arrived = lax.all_to_all(blocks[asked], "seq", split_axis=0, concat_axis=0, tiled=True)
    keys = arrived.reshape(slot_total * BLOCK_LEN, width)
    keys_lat = keys[:, :latent]
    q_lat = jnp.einsum("qhn,hnl->qhl", q_nope, weight_k, preferred_element_type=jnp.float32).astype(
        jnp.bfloat16
    )
    qfull = jnp.concatenate([q_lat, q_rope], axis=-1)
    chosen = jnp.any(
        sel[:, :, None] == jnp.arange(slot_total, dtype=jnp.int32)[None, None, :], axis=1
    )
    live = jnp.repeat(chosen, BLOCK_LEN, axis=1)[:, None, :]
    score = jnp.einsum("qhc,tc->qht", qfull, keys, preferred_element_type=jnp.float32) * scale
    score = jnp.where(live, score, -jnp.inf)
    prob = jax.nn.softmax(score, axis=-1)
    prob_low = prob.astype(jnp.bfloat16)
    olat = jnp.einsum("qht,tl->qhl", prob_low, keys_lat, preferred_element_type=jnp.float32).astype(
        jnp.bfloat16
    )
    attn_out = jnp.einsum(
        "qhl,hlv->qhv", olat, weight_v, preferred_element_type=jnp.float32
    ).astype(jnp.bfloat16)
    d_olat = jnp.einsum("qhv,hlv->qhl", d_out, weight_v, preferred_element_type=jnp.float32).astype(
        jnp.bfloat16
    )
    dprob = jnp.einsum("qhl,tl->qht", d_olat, keys_lat, preferred_element_type=jnp.float32)
    delta = jnp.sum(prob * dprob, axis=-1, keepdims=True)
    dscore = (prob * (dprob - delta) * scale).astype(jnp.bfloat16)
    dquery = jnp.einsum("qht,tc->qhc", dscore, keys, preferred_element_type=jnp.float32)
    d_q_rope = dquery[:, :, latent:].astype(jnp.bfloat16)
    d_qlat = dquery[:, :, :latent].astype(jnp.bfloat16)
    d_q_nope = jnp.einsum(
        "qhl,hnl->qhn", d_qlat, weight_k, preferred_element_type=jnp.float32
    ).astype(jnp.bfloat16)
    value_part = jnp.einsum("qht,qhl->tl", prob_low, d_olat, preferred_element_type=jnp.float32)
    dkeys = jnp.einsum("qht,qhc->tc", dscore, qfull, preferred_element_type=jnp.float32)
    dkeys = dkeys + jnp.pad(value_part, ((0, 0), (0, rope)))
    one_hot = (
        asked.reshape(-1)[:, None] == jnp.arange(own_blocks, dtype=jnp.int32)[None, :]
    ).astype(jnp.float32)
    returned = lax.all_to_all(
        dkeys.reshape(peers, per_peer, BLOCK_LEN * width).astype(jnp.bfloat16),
        "seq",
        split_axis=0,
        concat_axis=0,
        tiled=True,
    ).astype(jnp.float32)
    local_grad = jnp.dot(
        one_hot.T,
        returned.reshape(peers * per_peer, BLOCK_LEN * width),
        precision=lax.Precision.HIGHEST,
    )
    d_cache = (
        lax.psum(local_grad.astype(jnp.bfloat16), "grp")
        .astype(jnp.float32)
        .reshape(own_blocks * BLOCK_LEN, width)
    )
    return (attn_out, d_q_nope, d_q_rope, d_cache)


def solution(mesh):
    return jax.shard_map(
        local,
        mesh=mesh,
        in_specs=(
            P("seq", "grp", None),
            P("seq", "grp", None),
            P("seq", None),
            P("grp", "seq"),
            P("grp", "seq"),
            P("seq", "grp", None),
            P("seq", None),
            P("seq", None),
        ),
        out_specs=(
            P("seq", "grp", None),
            P("seq", "grp", None),
            P("seq", "grp", None),
            P("seq", None),
        ),
        check_vma=False,
    )
```

profile of v0, /device:TPU:8, one launch (start us, length us, event | category | flops | bytes accessed | tf_op | source)
XLA Modules:
  0.0 523.4 jit_solution(6179962597997448510)
XLA Ops:
  7.9 1.4 copy.80
  9.3 12.1 %all-to-all-start = ((s32[64,1,1]{2,1,0:T(1,128)}), s32[64,1,1]{2,1,0:T(1,128)S(1)}, u32[]{:S(2)}, u32[]{:S(2)}) async-start(s32[64,1,1]{2,1,0:T(1,128)} %copy.80), calls=%async_computation | async-start | bytes 65536 | tf_op jit(solution)/shard_map/all_to_all | solution.py:28
  21.4 1.7 copy.79
  23.1 6.9 %all-to-all-done = s32[64,1,1]{2,1,0:T(1,128)S(1)} async-done(((s32[64,1,1]{2,1,0:T(1,128)}), s32[64,1,1]{2,1,0:T(1,128)S(1)}, u32[]{:S(2)}, u32[]{:S(2)}) %all-to-all-start) | async-done | bytes 288 | tf_op jit(solution)/shard_map/all_to_all | solution.py:28
  29.9 2.4 fusion.49
  32.3 3.5 gather_fusion
  35.8 6.7 %all-to-all-start.1 = ((bf16[64,1,64,576]{3,2,1,0:T(8,128)(2,1)}), bf16[64,1,64,576]{3,2,1,0:T(8,128)(2,1)}, u32[]{:S(2)}, u32[]{:S(2)}) async-start(bf16[64,1,64,576]{3,2,1,0:T(8,128)(2,1)} %bitcast.47), calls=%async_computation.1 | async-start | bytes 10485760 | tf_op jit(solution)/shard_map/all_to_all | solution.py:30
  43.9 67.8 %all-gather.5.cloned.1.call-done = bf16[32,65536]{1,0:T(8,128)(2,1)} async-done(((bf16[32,1024]{1,0:T(8,128)(2,1)}), bf16[32,65536]{1,0:T(8,128)(2,1)}) %all-gather.5.cloned.1.call-update) | async-done | bytes 4194320 | tf_op jit(solution)/shard_map/all_gather | solution.py:23
  111.7 5.1 copy.102
  116.8 78.3 %all-gather.3.cloned.1.call-done = bf16[32,65536]{1,0:T(8,128)(2,1)} async-done(((bf16[32,1024]{1,0:T(8,128)(2,1)}), bf16[32,65536]{1,0:T(8,128)(2,1)}) %all-gather.3.cloned.1.call-update) | async-done | bytes 4194320 | tf_op jit(solution)/shard_map/all_gather | solution.py:22
  195.1 3.9 copy.101
  199.0 2.1 copy-done.3
  201.8 1.2 fusion.27
  203.0 8.0 %fusion.12 = f32[16,32,4096]{2,1,0:T(8,128)} fusion(bf16[4096,576]{1,0:T(8,128)(2,1)} %bitcast.5, bf16[16,32,512]{2,0,1:T(8,128)(2,1)S(1)} %fusion.27), kind=kOutput, calls=%fused_computation.20 | convolution fusion | flops 2147483648 | bytes 13107200 | tf_op jit(solution)/shard_map/qhl,tl->qht/dot_general | solution.py:54
  211.0 10.7 %fusion.50 = (f32[16,32]{1,0:T(8,128)S(1)}, f32[16,32,4096]{2,1,0:T(8,128)}) fusion(pred[16,4096]{1,0:T(8,128)(4,1)S(1)} %broadcast_in_dim.25, bf16[4096,576,1]{1,0,2:T(8,128)(2,1)} %bitcast.6, bf16[16,32,576]{2,0,1:T(8,128)(2,1)S(1)} %pad_maximum_fusion), kind=kOutput, calls=%fused_computation.59 | convolution fusion | flops 2424311808 | bytes 13764608 | tf_op jit(solution)/shard_map/sub | solution.py:43
  221.7 9.4 %convolution_bitcast_fusion = f32[4096,512]{0,1:T(8,128)} fusion(bf16[16,32,512]{2,0,1:T(8,128)(2,1)S(1)} %fusion.27, f32[16,32,4096]{2,1,0:T(8,128)} %get-tuple-element.27, f32[16,32]{1,0:T(8,128)S(1)} %get-tuple-element.26), kind=kOutput, calls=%fused_computation.12 | convolution fusion | flops 2151677952 | bytes 17303552 | tf_op jit(solution)/shard_map/qht,qhl->tl/dot_general | solution.py:63
  231.1 18.8 %fusion.2 = bf16[4096,576]{0,1:T(8,128)(2,1)} fusion(f32[4096,512]{0,1:T(8,128)} %convolution_bitcast_fusion, f32[16,32,4096]{2,1,0:T(8,128)} %fusion.12, bf16[16,32,576]{2,0,1:T(8,128)(2,1)S(1)} %pad_maximum_fusion, f32[16,32,4096]{2,1,0:T(8,128)} %get-tuple-element.27, f32[16,32]{1,0:T(8,128)S(1)} %get-tuple-element.26), kind=kOutput, calls=%fused_computation.5 | convolution fusion | flops 2435322368 | bytes 30476288 | tf_op jit(solution)/shard_map/qht,qhc->tc/dot_general | solution.py:64
  249.9 7.6 %copy.91 = bf16[4096,576]{1,0:T(8,128)(2,1)} copy(bf16[4096,576]{0,1:T(8,128)(2,1)} %fusion.2) | data formatting | bytes 9437184 | tf_op jit(solution)/shard_map/convert_element_type | solution.py:70
  257.5 21.7 %convert_element_type.71 = bf16[64,1,36864]{2,1,0:T(2,128)(2,1)} reshape(bf16[4096,576]{1,0:T(8,128)(2,1)} %copy.91) | data formatting | bytes 9437184 | tf_op jit(solution)/shard_map/convert_element_type | solution.py:70
  279.7 29.9 %reduce.4 = bf16[64,36864]{1,0:T(8,128)(2,1)} reduce(bf16[64,1,36864]{2,1,0:T(2,128)(2,1)} %convert_element_type.71, bf16[]{:T(256)} %broadcast.36), dimensions={1}, to_apply=%convert_element_type.71.reduce_sub_computation | reduce | bytes 9437186 | tf_op jit(solution)/shard_map/convert_element_type | solution.py:70
  309.7 8.3 %reshape.84 = bf16[64,2,18432]{2,1,0:T(2,128)(2,1)} reshape(bf16[64,36864]{1,0:T(8,128)(2,1)} %reduce.4) | data formatting | bytes 9437184
  317.9 8.0 %all-to-all-start.2 = ((bf16[64,2,18432]{2,1,0:T(2,128)(2,1)}), bf16[64,2,18432]{2,1,0:T(2,128)(2,1)}, u32[]{:S(2)}, u32[]{:S(2)}) async-start(bf16[64,2,18432]{2,1,0:T(2,128)(2,1)} %reshape.84), calls=%async_computation.2 | async-start | bytes 9437184 | tf_op jit(solution)/shard_map/all_to_all | solution.py:69
  326.2 7.0 %fusion.24 = bf16[16,32,512]{2,1,0:T(8,128)(2,1)S(1)} fusion(bf16[4096,576]{1,0:T(8,128)(2,1)} %bitcast.5, f32[16,32,4096]{2,1,0:T(8,128)} %get-tuple-element.27, f32[16,32]{1,0:T(8,128)S(1)} %get-tuple-element.26), kind=kOutput, calls=%fused_computation.26 | convolution fusion | flops 2151940096 | bytes 13109248 | tf_op jit(solution)/shard_map/qht,tl->qhl/dot_general | solution.py:45
  333.2 100.1 %all-to-all-done.2 = bf16[64,2,18432]{2,1,0:T(2,128)(2,1)} async-done(((bf16[64,2,18432]{2,1,0:T(2,128)(2,1)}), bf16[64,2,18432]{2,1,0:T(2,128)(2,1)}, u32[]{:S(2)}, u32[]{:S(2)}) %all-to-all-start.2) | async-done | bytes 4718624 | tf_op jit(solution)/shard_map/all_to_all | solution.py:69
  433.3 20.2 %reshape.85 = bf16[64,1,36864]{2,1,0:T(2,128)(2,1)} reshape(bf16[64,2,18432]{2,1,0:T(2,128)(2,1)} %all-to-all-done.2) | data formatting | bytes 9437184
  453.4 8.8 %convolution_convert_fusion = bf16[16,36864]{1,0:T(8,128)(2,1)S(1)} fusion(bf16[64,1,36864]{2,1,0:T(2,128)(2,1)} %reshape.85, s32[64]{0:T(128)S(1)} %get-tuple-element.24), kind=kOutput, calls=%fused_computation.3 | convolution fusion | flops 76088320 | bytes 5898496 | tf_op jit(solution)/shard_map/dot_general | solution.py:76
  462.2 2.5 reshape.67
  464.7 14.8 %fusion.21 = bf16[16,32,576]{2,1,0:T(8,128)(2,1)S(1)} fusion(bf16[4096,576,1]{1,0,2:T(8,128)(2,1)} %bitcast.6, f32[16,32,4096]{2,1,0:T(8,128)} %fusion.12, f32[16,32,4096]{2,1,0:T(8,128)} %get-tuple-element.27, f32[16,32]{1,0:T(8,128)S(1)} %get-tuple-element.26), kind=kOutput, calls=%fused_computation.25 | convolution fusion | flops 2430898688 | bytes 22087680 | tf_op jit(solution)/shard_map/qht,tc->qhc/dot_general | solution.py:57
  480.2 3.5 fusion.29
  484.4 1.2 fusion.30
  486.3 27.6 %all-reduce.3.cloned.1.call-done = bf16[1024,576]{1,0:T(8,128)(2,1)} async-done(((bf16[1024,576]{1,0:T(8,128)(2,1)}), bf16[1024,576]{1,0:T(8,128)(2,1)}) %all-reduce.3.cloned.1.call-update) | async-done | bytes 1179664 | tf_op jit(solution)/shard_map/psum | solution.py:82
  513.9 2.7 copy.95
  (34 shorter events, 5.8 us)
Async XLA Ops:
  7.2 194.6 %copy-start = (bf16[16,32,128]{2,1,0:T(8,128)(2,1)S(1)}, bf16[16,32,128]{2,1,0:T(8,128)(2,1)}, u32[]{:S(2)}) copy-start(bf16[16,32,128]{2,1,0:T(8,128)(2,1)} %param.13) | copy-start | bytes 393220
  7.2 104.5 %all-gather.5.cloned.1.call-start = ((), (), s32[]{:S(2)}) async-start(), calls=%async_computation.4 | async-start | bytes 4259840 | tf_op jit(solution)/shard_map/all_gather | solution.py:23
  9.3 20.7 %all-to-all-start = ((s32[64,1,1]{2,1,0:T(1,128)}), s32[64,1,1]{2,1,0:T(1,128)S(1)}, u32[]{:S(2)}, u32[]{:S(2)}) async-start(s32[64,1,1]{2,1,0:T(1,128)} %copy.80), calls=%async_computation | async-start | bytes 65536 | tf_op jit(solution)/shard_map/all_to_all | solution.py:28
  35.8 7.4 %copy-start.7 = (s32[16,32]{1,0:T(8,128)S(1)}, s32[16,32]{1,0:T(8,128)}, u32[]{:S(2)}) copy-start(s32[16,32]{1,0:T(8,128)} %param.14) | copy-start | bytes 6148
  35.8 8.0 %copy-start.6 = (bf16[16,32,64]{2,1,0:T(8,128)(2,1)S(1)}, bf16[16,32,64]{2,1,0:T(8,128)(2,1)}, u32[]{:S(2)}) copy-start(bf16[16,32,64]{2,1,0:T(8,128)(2,1)} %param.9) | copy-start | bytes 196612
  35.8 167.2 %all-to-all-start.1 = ((bf16[64,1,64,576]{3,2,1,0:T(8,128)(2,1)}), bf16[64,1,64,576]{3,2,1,0:T(8,128)(2,1)}, u32[]{:S(2)}, u32[]{:S(2)}) async-start(bf16[64,1,64,576]{3,2,1,0:T(8,128)(2,1)} %bitcast.47), calls=%async_computation.1 | async-start | bytes 10485760 | tf_op jit(solution)/shard_map/all_to_all | solution.py:30
  42.5 152.7 %all-gather.3.cloned.1.call-start = ((), (), s32[]{:S(2)}) async-start(), calls=%async_computation.3 | async-start | bytes 4259840 | tf_op jit(solution)/shard_map/all_gather | solution.py:22
  116.8 84.3 %copy-start.5 = (bf16[16,32,128]{2,1,0:T(8,128)(2,1)S(1)}, bf16[16,32,128]{2,1,0:T(8,128)(2,1)}, u32[]{:S(2)}) copy-start(bf16[16,32,128]{2,1,0:T(8,128)(2,1)} %param.8) | copy-start | bytes 393220
  195.1 6.7 %copy-start.2 = (bf16[4,8,512,128]{3,2,1,0:T(8,128)(2,1)S(1)}, bf16[4,8,512,128]{3,2,1,0:T(8,128)(2,1)}, u32[]{:S(2)}) copy-start(bf16[4,8,512,128]{3,2,1,0:T(8,128)(2,1)} %copy.102) | copy-start | bytes 12582916
  199.0 2.1 copy-start.3
  317.9 115.3 %all-to-all-start.2 = ((bf16[64,2,18432]{2,1,0:T(2,128)(2,1)}), bf16[64,2,18432]{2,1,0:T(2,128)(2,1)}, u32[]{:S(2)}, u32[]{:S(2)}) async-start(bf16[64,2,18432]{2,1,0:T(2,128)(2,1)} %reshape.84), calls=%async_computation.2 | async-start | bytes 9437184 | tf_op jit(solution)/shard_map/all_to_all | solution.py:69
  325.9 188.0 %all-reduce.3.cloned.1.call-start = ((), (), s32[]{:S(2)}) async-start(), calls=%async_computation.5 | async-start | bytes 2621440 | tf_op jit(solution)/shard_map/psum | solution.py:82
  479.5 5.0 copy-start.4
  480.2 36.4 %copy-start.1 = (bf16[16,32,128]{2,1,0:T(8,128)(2,1)S(1)}, bf16[16,32,128]{2,1,0:T(8,128)(2,1)}, u32[]{:S(2)}) copy-start(bf16[16,32,128]{2,1,0:T(8,128)(2,1)} %param.13) | copy-start | bytes 393220
Sparse Core Ops, SparseCore 0:
  10.8 100.8 all-gather.4
  114.5 80.5 all-gather.2
  464.8 49.0 all-reduce.2
where the time goes:
time: 529 us; the launch traced here: 523 us
  waiting for transfers between devices  282 us (53%)
  matrix products  84 us (16%)
  local copies, waits for them, and re-layouts  83.7 us (16%)
  other arithmetic  32.5 us (6%)
  starting transfers between devices  27.5 us (5%)
  between operations  14.1 us (3%)
    all_to_all x1, waiting for transfers between devices, local(): lax.all_to_all(dkeys.reshape(peers, per_peer, BLOCK_LEN * width).astype(j...  100 us
    all_gather x1, waiting for transfers between devices, local(): lax.all_gather(w_uk, 'seq', axis=1, tiled=True)  78.3 us
    all_gather x1, waiting for transfers between devices, local(): lax.all_gather(w_uv, 'seq', axis=1, tiled=True)  67.8 us
    unnamed x25, local copies, waits for them, and re-layouts  45.4 us
    convert_element_type x1, other arithmetic, local(): dkeys.reshape(peers, per_peer, BLOCK_LEN * width).astype(jnp.bfloat16)  29.9 us
    convert_element_type x3, local copies, waits for them, and re-layouts, local(): dkeys.reshape(peers, per_peer, BLOCK_LEN * width).astype(jnp.bfloat16)  29.9 us
    psum x1, waiting for transfers between devices, local(): lax.psum(local_grad.astype(jnp.bfloat16), 'grp').astype(jnp.float32)  27.6 us
    dot_general x1, matrix products, local(): jnp.einsum('qht,qhc->tc', dscore, qfull, preferred_element_type=jnp.float32)  18.8 us
  transfers between devices with their start and end apart: 6, of which 5 were waited for; matrix products, arithmetic and copies ran while one was open for 9% of the time, Pallas kernels for 0%

commit v1 on v0

--- a/solution.py
+++ b/solution.py
@@ -5,6 +5,7 @@
 from jax.sharding import PartitionSpec as P
 
 BLOCK_LEN = 64
+extend_the_group = lambda chunk: jnp.sum(lax.all_gather(chunk, axis_name="grp"), axis=0)
 
 
 def local(q_nope, q_rope, cache, w_uk, w_uv, d_out, sel, slot_blocks):
@@ -79,7 +80,7 @@
         precision=lax.Precision.HIGHEST,
     )
     d_cache = (
-        lax.psum(local_grad.astype(jnp.bfloat16), "grp")
+        extend_the_group(local_grad.astype(jnp.bfloat16))
         .astype(jnp.float32)
         .reshape(own_blocks * BLOCK_LEN, width)
     )

time: 529 us -> 539 us (1.019)
  blocking collectives: 0 us -> 115 us
  waiting for transfers between devices: 282 us -> 180 us
  starting transfers between devices: 27.5 us -> 19.2 us
    all_to_all x0 -> x1, blocking collectives: none -> 115 us  [local(): lax.all_to_all(dkeys.reshape(peers, per_peer, BLOCK_LEN * width).astype(j...]
    all_to_all x1 -> x0, waiting for transfers between devices: 100 us -> none  [local(): lax.all_to_all(dkeys.reshape(peers, per_peer, BLOCK_LEN * width).astype(j...]
    psum x1 -> x0, waiting for transfers between devices: 27.6 us -> none  [local(): lax.psum(local_grad.astype(jnp.bfloat16), 'grp').astype(jnp.float32)]
    all_gather x0 -> x1, waiting for transfers between devices: none -> 23.7 us  [lax.all_gather(chunk, axis_name='grp')]
    all_to_all x1 -> x0, starting transfers between devices: 7.96 us -> none  [local(): lax.all_to_all(dkeys.reshape(peers, per_peer, BLOCK_LEN * width).astype(j...]
    unnamed x25 -> x27, local copies, waits for them, and re-layouts: 45.4 us -> 45.4 us
  transfers between devices with their start and end apart: 6 -> 5, of which waited for: 5 -> 4; matrix products, arithmetic and copies ran while one was open for 9% -> 9% of each run, Pallas kernels for 0% -> 0%
where the time goes in v1:
time: 539 us; the launch traced here: 533 us
  waiting for transfers between devices  180 us (33%)
  blocking collectives  115 us (21%)
  matrix products  84 us (16%)
  local copies, waits for them, and re-layouts  83.7 us (16%)
  other arithmetic  36.9 us (7%)
  starting transfers between devices  19.2 us (4%)
  between operations  14.1 us (3%)
    all_to_all x1, blocking collectives, local(): lax.all_to_all(dkeys.reshape(peers, per_peer, BLOCK_LEN * width).astype(j...  115 us
    all_gather x1, waiting for transfers between devices, local(): lax.all_gather(w_uk, 'seq', axis=1, tiled=True)  80.1 us
    all_gather x1, waiting for transfers between devices, local(): lax.all_gather(w_uv, 'seq', axis=1, tiled=True)  67.6 us
    unnamed x27, local copies, waits for them, and re-layouts  45.4 us
    convert_element_type x1, other arithmetic, local(): dkeys.reshape(peers, per_peer, BLOCK_LEN * width).astype(jnp.bfloat16)  29.9 us
    convert_element_type x3, local copies, waits for them, and re-layouts, local(): dkeys.reshape(peers, per_peer, BLOCK_LEN * width).astype(jnp.bfloat16)  29.9 us
    all_gather x1, waiting for transfers between devices, lax.all_gather(chunk, axis_name='grp')  23.7 us
    dot_general x1, matrix products, local(): jnp.einsum('qht,qhc->tc', dscore, qfull, preferred_element_type=jnp.float32)  18.8 us
  transfers between devices with their start and end apart: 5, of which 4 were waited for; matrix products, arithmetic and copies ran while one was open for 9% of the time, Pallas kernels for 0%

profile of v1, /device:TPU:8, one launch (start us, length us, event | category | flops | bytes accessed | tf_op | source)
XLA Modules:
  0.0 532.9 jit_solution(2566794556627996939)
XLA Ops:
  7.9 1.4 copy.79
  9.3 12.1 %all-to-all-start = ((s32[64,1,1]{2,1,0:T(1,128)}), s32[64,1,1]{2,1,0:T(1,128)S(1)}, u32[]{:S(2)}, u32[]{:S(2)}) async-start(s32[64,1,1]{2,1,0:T(1,128)} %copy.79), calls=%async_computation | async-start | bytes 65536 | tf_op jit(solution)/shard_map/all_to_all | solution.py:29
  21.4 1.7 copy.78
  23.1 6.9 %all-to-all-done = s32[64,1,1]{2,1,0:T(1,128)S(1)} async-done(((s32[64,1,1]{2,1,0:T(1,128)}), s32[64,1,1]{2,1,0:T(1,128)S(1)}, u32[]{:S(2)}, u32[]{:S(2)}) %all-to-all-start) | async-done | bytes 288 | tf_op jit(solution)/shard_map/all_to_all | solution.py:29
  29.9 2.4 fusion.49
  32.3 3.5 gather_fusion
  35.8 6.6 %all-to-all-start.1 = ((bf16[64,1,64,576]{3,2,1,0:T(8,128)(2,1)}), bf16[64,1,64,576]{3,2,1,0:T(8,128)(2,1)}, u32[]{:S(2)}, u32[]{:S(2)}) async-start(bf16[64,1,64,576]{3,2,1,0:T(8,128)(2,1)} %bitcast.48), calls=%async_computation.1 | async-start | bytes 10485760 | tf_op jit(solution)/shard_map/all_to_all | solution.py:31
  44.2 67.6 %all-gather.7.cloned.1.call-done = bf16[32,65536]{1,0:T(8,128)(2,1)} async-done(((bf16[32,1024]{1,0:T(8,128)(2,1)}), bf16[32,65536]{1,0:T(8,128)(2,1)}) %all-gather.7.cloned.1.call-update) | async-done | bytes 4194320 | tf_op jit(solution)/shard_map/all_gather | solution.py:24
  111.8 5.2 copy.101
  117.0 80.1 %all-gather.5.cloned.1.call-done = bf16[32,65536]{1,0:T(8,128)(2,1)} async-done(((bf16[32,1024]{1,0:T(8,128)(2,1)}), bf16[32,65536]{1,0:T(8,128)(2,1)}) %all-gather.5.cloned.1.call-update) | async-done | bytes 4194320 | tf_op jit(solution)/shard_map/all_gather | solution.py:23
  197.0 3.9 copy.100
  200.9 2.1 copy-done.4
  203.8 1.2 fusion.27
  204.9 8.0 %fusion.12 = f32[16,32,4096]{2,1,0:T(8,128)} fusion(bf16[4096,576]{1,0:T(8,128)(2,1)} %bitcast.5, bf16[16,32,512]{2,0,1:T(8,128)(2,1)S(1)} %fusion.27), kind=kOutput, calls=%fused_computation.20 | convolution fusion | flops 2147483648 | bytes 13107200 | tf_op jit(solution)/shard_map/qhl,tl->qht/dot_general | solution.py:55
  212.9 10.7 %fusion.50 = (f32[16,32]{1,0:T(8,128)S(1)}, f32[16,32,4096]{2,1,0:T(8,128)}) fusion(pred[16,4096]{1,0:T(8,128)(4,1)S(1)} %broadcast_in_dim.25, bf16[4096,576,1]{1,0,2:T(8,128)(2,1)} %bitcast.6, bf16[16,32,576]{2,0,1:T(8,128)(2,1)S(1)} %pad_maximum_fusion), kind=kOutput, calls=%fused_computation.59 | convolution fusion | flops 2424311808 | bytes 13764608 | tf_op jit(solution)/shard_map/sub | solution.py:44
  223.6 9.8 %convolution_bitcast_fusion = f32[4096,512]{0,1:T(8,128)} fusion(bf16[16,32,512]{2,0,1:T(8,128)(2,1)S(1)} %fusion.27, f32[16,32,4096]{2,1,0:T(8,128)} %get-tuple-element.27, f32[16,32]{1,0:T(8,128)S(1)} %get-tuple-element.26), kind=kOutput, calls=%fused_computation.12 | convolution fusion | flops 2151677952 | bytes 17303552 | tf_op jit(solution)/shard_map/qht,qhl->tl/dot_general | solution.py:64
  233.4 18.8 %fusion.2 = bf16[4096,576]{0,1:T(8,128)(2,1)} fusion(f32[4096,512]{0,1:T(8,128)} %convolution_bitcast_fusion, f32[16,32,4096]{2,1,0:T(8,128)} %fusion.12, bf16[16,32,576]{2,0,1:T(8,128)(2,1)S(1)} %pad_maximum_fusion, f32[16,32,4096]{2,1,0:T(8,128)} %get-tuple-element.27, f32[16,32]{1,0:T(8,128)S(1)} %get-tuple-element.26), kind=kOutput, calls=%fused_computation.5 | convolution fusion | flops 2435322368 | bytes 30476288 | tf_op jit(solution)/shard_map/qht,qhc->tc/dot_general | solution.py:65
  252.2 7.6 %copy.90 = bf16[4096,576]{1,0:T(8,128)(2,1)} copy(bf16[4096,576]{0,1:T(8,128)(2,1)} %fusion.2) | data formatting | bytes 9437184 | tf_op jit(solution)/shard_map/convert_element_type | solution.py:71
  259.8 21.7 %convert_element_type.82 = bf16[64,1,36864]{2,1,0:T(2,128)(2,1)} reshape(bf16[4096,576]{1,0:T(8,128)(2,1)} %copy.90) | data formatting | bytes 9437184 | tf_op jit(solution)/shard_map/convert_element_type | solution.py:71
  282.0 29.9 %reduce.5 = bf16[64,36864]{1,0:T(8,128)(2,1)} reduce(bf16[64,1,36864]{2,1,0:T(2,128)(2,1)} %convert_element_type.82, bf16[]{:T(256)} %broadcast.36), dimensions={1}, to_apply=%convert_element_type.82.reduce_sub_computation | reduce | bytes 9437186 | tf_op jit(solution)/shard_map/convert_element_type | solution.py:71
  312.0 8.2 %reshape.82 = bf16[64,2,18432]{2,1,0:T(2,128)(2,1)} reshape(bf16[64,36864]{1,0:T(8,128)(2,1)} %reduce.5) | data formatting | bytes 9437184
  320.2 115.3 %all_to_all.19 = bf16[64,2,18432]{2,1,0:T(2,128)(2,1)} all-to-all(bf16[64,2,18432]{2,1,0:T(2,128)(2,1)} %reshape.82), channel_id=1, replica_groups=mesh['seq'=64,'grp'=4] {'seq'}, dimensions={0} | all-to-all | bytes 9437184 | tf_op jit(solution)/shard_map/all_to_all | solution.py:70
  435.5 20.1 %reshape.83 = bf16[64,1,36864]{2,1,0:T(2,128)(2,1)} reshape(bf16[64,2,18432]{2,1,0:T(2,128)(2,1)} %all_to_all.19) | data formatting | bytes 9437184
  455.7 9.8 %convolution_convert_fusion = bf16[16,36864]{1,0:T(8,128)(2,1)} fusion(bf16[64,1,36864]{2,1,0:T(2,128)(2,1)} %reshape.83, s32[64]{0:T(128)S(1)} %get-tuple-element.24), kind=kOutput, calls=%fused_computation.3 | convolution fusion | flops 76088320 | bytes 5898496 | tf_op jit(solution)/shard_map/dot_general | solution.py:77
  465.5 15.9 %fusion.21 = bf16[16,32,576]{2,1,0:T(8,128)(2,1)S(1)} fusion(bf16[4096,576,1]{1,0,2:T(8,128)(2,1)} %bitcast.6, f32[16,32,4096]{2,1,0:T(8,128)} %fusion.12, f32[16,32,4096]{2,1,0:T(8,128)} %get-tuple-element.27, f32[16,32]{1,0:T(8,128)S(1)} %get-tuple-element.26), kind=kOutput, calls=%fused_computation.25 | convolution fusion | flops 2430898688 | bytes 22087680 | tf_op jit(solution)/shard_map/qht,tc->qhc/dot_general | solution.py:58
  482.1 7.2 %fusion.24 = bf16[16,32,512]{2,1,0:T(8,128)(2,1)S(1)} fusion(bf16[4096,576]{1,0:T(8,128)(2,1)} %bitcast.5, f32[16,32,4096]{2,1,0:T(8,128)} %get-tuple-element.27, f32[16,32]{1,0:T(8,128)S(1)} %get-tuple-element.26), kind=kOutput, calls=%fused_computation.26 | convolution fusion | flops 2151940096 | bytes 13109248 | tf_op jit(solution)/shard_map/qht,tl->qhl/dot_general | solution.py:46
  489.3 0.9 fusion.29
  491.7 1.2 fusion.30
  493.6 23.7 %all-gather.9.cloned.1.call-done = bf16[64,36864]{1,0:T(8,128)(2,1)} async-done(((bf16[16,36864]{1,0:T(8,128)(2,1)}), bf16[64,36864]{1,0:T(8,128)(2,1)}) %all-gather.9.cloned.1.call-update) | async-done | bytes 4718608 | tf_op jit(solution)/shard_map/all_gather | solution.py:8
  517.3 4.4 reduce_sum.32
  521.7 2.4 reshape.65
  524.1 2.0 copy.94
  (36 shorter events, 6.6 us)
Async XLA Ops:
  7.2 196.6 %copy-start = (bf16[16,32,128]{2,1,0:T(8,128)(2,1)S(1)}, bf16[16,32,128]{2,1,0:T(8,128)(2,1)}, u32[]{:S(2)}) copy-start(bf16[16,32,128]{2,1,0:T(8,128)(2,1)} %param.13) | copy-start | bytes 393220
  7.2 104.6 %all-gather.7.cloned.1.call-start = ((), (), s32[]{:S(2)}) async-start(), calls=%async_computation.4 | async-start | bytes 4259840 | tf_op jit(solution)/shard_map/all_gather | solution.py:24
  9.3 20.7 %all-to-all-start = ((s32[64,1,1]{2,1,0:T(1,128)}), s32[64,1,1]{2,1,0:T(1,128)S(1)}, u32[]{:S(2)}, u32[]{:S(2)}) async-start(s32[64,1,1]{2,1,0:T(1,128)} %copy.79), calls=%async_computation | async-start | bytes 65536 | tf_op jit(solution)/shard_map/all_to_all | solution.py:29
  35.8 7.7 %copy-start.8 = (s32[16,32]{1,0:T(8,128)S(1)}, s32[16,32]{1,0:T(8,128)}, u32[]{:S(2)}) copy-start(s32[16,32]{1,0:T(8,128)} %param.14) | copy-start | bytes 6148
  35.8 8.4 %copy-start.7 = (bf16[16,32,64]{2,1,0:T(8,128)(2,1)S(1)}, bf16[16,32,64]{2,1,0:T(8,128)(2,1)}, u32[]{:S(2)}) copy-start(bf16[16,32,64]{2,1,0:T(8,128)(2,1)} %param.9) | copy-start | bytes 196612
  35.8 169.2 %all-to-all-start.1 = ((bf16[64,1,64,576]{3,2,1,0:T(8,128)(2,1)}), bf16[64,1,64,576]{3,2,1,0:T(8,128)(2,1)}, u32[]{:S(2)}, u32[]{:S(2)}) async-start(bf16[64,1,64,576]{3,2,1,0:T(8,128)(2,1)} %bitcast.48), calls=%async_computation.1 | async-start | bytes 10485760 | tf_op jit(solution)/shard_map/all_to_all | solution.py:31
  42.4 154.6 %all-gather.5.cloned.1.call-start = ((), (), s32[]{:S(2)}) async-start(), calls=%async_computation.3 | async-start | bytes 4259840 | tf_op jit(solution)/shard_map/all_gather | solution.py:23
  43.2 474.1 %all-gather.9.cloned.1.call-start = ((), (), s32[]{:S(2)}) async-start(), calls=%async_computation.5 | async-start | bytes 5898240 | tf_op jit(solution)/shard_map/all_gather | solution.py:8
  117.0 86.0 %copy-start.6 = (bf16[16,32,128]{2,1,0:T(8,128)(2,1)S(1)}, bf16[16,32,128]{2,1,0:T(8,128)(2,1)}, u32[]{:S(2)}) copy-start(bf16[16,32,128]{2,1,0:T(8,128)(2,1)} %param.8) | copy-start | bytes 393220
  197.0 6.7 %copy-start.2 = (bf16[4,8,512,128]{3,2,1,0:T(8,128)(2,1)S(1)}, bf16[4,8,512,128]{3,2,1,0:T(8,128)(2,1)}, u32[]{:S(2)}) copy-start(bf16[4,8,512,128]{3,2,1,0:T(8,128)(2,1)} %copy.101) | copy-start | bytes 12582916
  200.9 2.1 copy-start.4
  482.1 7.2 %copy-start.3 = (bf16[4,8,512,128]{3,2,1,0:T(8,128)(2,1)S(1)}, bf16[4,8,512,128]{3,2,1,0:T(8,128)(2,1)}, u32[]{:S(2)}) copy-start(bf16[4,8,512,128]{3,2,1,0:T(8,128)(2,1)} %copy.101) | copy-start | bytes 12582916
  489.3 2.3 copy-start.5
  517.3 8.8 %copy-start.1 = (bf16[16,32,128]{2,1,0:T(8,128)(2,1)S(1)}, bf16[16,32,128]{2,1,0:T(8,128)(2,1)}, u32[]{:S(2)}) copy-start(bf16[16,32,128]{2,1,0:T(8,128)(2,1)} %param.13) | copy-start | bytes 393220
Sparse Core Ops, SparseCore 0:
  10.8 100.9 all-gather.6
  114.6 82.3 all-gather.4
  465.6 51.6 all-gather.8
